TPU v7x, 32 devices: a whole 2x2x4 slice. The times are simulated.
32 devices in a mesh: dp: 8 (over y, x, core), seq: 4 (over z).
Axes of the slice: x: 2, y: 2, z: 4, core: 2. Of those that a mesh axis runs over, the one named last changes fastest.
Arguments:
- block_input: bfloat16 [24, 1024, 1024], P('dp', 'seq'), may hold values from -6 to 6
- seg_start: int32 [24, 1024], P('dp'), may hold values from 0 to 1023, as said below
- ln1_gain: float32 [1024], replicated, may hold values from 0.5 to 1.5
- ln1_bias: float32 [1024], replicated, may hold values from -1.75 to 1.75
- qkv_weight: bfloat16 [1024, 3072], P('dp'), may hold values from -0.1875 to 0.1875
- query_bias: float32 [1024], replicated, may hold values from -1.75 to 1.75
- value_bias: float32 [1024], replicated, may hold values from -1.75 to 1.75
- query_adapter_reduce: bfloat16 [1024, 4], replicated, may hold values from -0.1875 to 0.1875
- query_up: bfloat16 [4, 1024], replicated, may hold values from -0.1875 to 0.1875
- value_adapter_reduce: bfloat16 [1024, 4], replicated, may hold values from -0.1875 to 0.1875
- value_up: bfloat16 [4, 1024], replicated, may hold values from -0.1875 to 0.1875
- out_weight: bfloat16 [1024, 1024], P('dp'), may hold values from -0.75 to 0.75
- out_bias: float32 [1024], replicated, may hold values from -1.75 to 1.75
- ln2_gain: float32 [1024], replicated, may hold values from 0.5 to 1.5
- ln2_bias: float32 [1024], replicated, may hold values from -1.75 to 1.75
- fc_weight: bfloat16 [1024, 4096], P('dp'), may hold values from -0.1875 to 0.1875
- fc_bias: float32 [4096], replicated, may hold values from -1.75 to 1.75
- proj_weight: bfloat16 [4096, 1024], P('dp'), may hold values from -0.09375 to 0.09375
- proj_bias: float32 [1024], replicated, may hold values from -1.75 to 1.75
- grad_out: bfloat16 [24, 1024, 1024], P('dp', 'seq'), may hold values from -6 to 6
Outputs:
- block_output: bfloat16 [24, 1024, 1024], P('dp', 'seq')
- grad_input: float32 [24, 1024, 1024], P('dp', 'seq')
- grad_query_down: float32 [1024, 4], replicated
- grad_query_up: float32 [4, 1024], replicated
- grad_value_down: float32 [1024, 4], replicated
- grad_value_up: float32 [4, 1024], replicated
Inputs may be any that keep to these rules, and one draw needn't show every extreme that they name: `seg_start`: each entry is the first position of its token's document within the row: it is at most the token's own position, position 0 has 0, and equal entries form runs of consecutive tokens whose start is the entry itself. The last position of every row starts its own document. In every row one document begins within the row's first 1 / N of positions and ends within its last 1 / N, N being the number of devices along seq.
All inputs are finite; a program needn't handle non-finite values.
Results may differ from a plain program's by a relative error of at most 0.014.
Values may be sent and summed in bfloat16 or wider, within the bound.
A program may use at most 192 MiB of HBM per device.

v0:
```python
from functools import partial
import jax
import jax.numpy as jnp
from jax import lax
from jax.sharding import PartitionSpec as P

HEAD = 64
NORM_EPSILON = 1e-05
ADAPTER_SCALE = 8.0
MASKED = -1e30


def for_sending(value):

    def short(part):
        return part.astype(jnp.bfloat16) if part.dtype == jnp.float32 else part

    return jax.tree.map(short, value)


def norm_forward(row_values, norm_gain, norm_shift):
    average = jnp.mean(row_values, axis=-1, keepdims=True)
    centered = row_values - average
    inverse = lax.rsqrt(jnp.mean(centered * centered, axis=-1, keepdims=True) + NORM_EPSILON)
    normed = centered * inverse
    return (normed * norm_gain + norm_shift, normed, inverse)


def norm_backward(gradient, normed, inverse, norm_gain):
    scaled = gradient * norm_gain
    return inverse * (
        scaled
        - jnp.mean(scaled, axis=-1, keepdims=True)
        - normed * jnp.mean(scaled * normed, axis=-1, keepdims=True)
    )


def fold_with(left_side, total_sum, weight_piece):
    columns = lax.slice_in_dim(left_side, 0, weight_piece.shape[0], axis=1)
    return total_sum + jnp.dot(columns, weight_piece, preferred_element_type=jnp.float32)


def times_transposed(left_side, right_side):
    return lax.dot_general(
        left_side, right_side, (((1,), (1,)), ((), ())), preferred_element_type=jnp.float32
    )


def across_token_rows(left_side, right_side):
    return lax.dot_general(
        left_side, right_side, (((0,), (0,)), ((), ())), preferred_element_type=jnp.float32
    )


def map_with(left_side, weight_piece):
    return times_transposed(left_side, weight_piece)


def mask_for(document_starts, offset, block_rows, length):
    query_pos = offset + jnp.arange(block_rows, dtype=jnp.int32)
    key_pos = jnp.arange(length, dtype=jnp.int32)
    query_start = document_starts[offset : offset + block_rows]
    return (key_pos[None, :] <= query_pos[:, None]) & (key_pos[None, :] >= query_start[:, None])


def split_heads(head_layout):
    length = head_layout.shape[0]
    head_count = head_layout.shape[2] // HEAD
    return (
        head_layout[:, 0].reshape(length, head_count, HEAD),
        head_layout[:, 1].reshape(length, head_count, HEAD),
        head_layout[:, 2].reshape(length, head_count, HEAD),
    )


def attend_row(row_entry):
    head_layout, document_starts = row_entry
    query_heads, key_heads, value_heads = split_heads(head_layout)
    length = head_layout.shape[0]
    block_rows = min(512, length)
    score_scale = HEAD ** (-0.5)
    mixed_parts = []
    total_parts = []
    for offset in range(0, length, block_rows):
        allowed = mask_for(document_starts, offset, block_rows, length)
        scores = (
            jnp.einsum(
                "qhd,khd->hqk",
                query_heads[offset : offset + block_rows],
                key_heads,
                preferred_element_type=jnp.float32,
            )
            * score_scale
        )
        scores = jnp.where(allowed[None], scores, MASKED)
        highest = jnp.max(scores, axis=-1, keepdims=True)
        weights = jnp.exp(scores - highest)
        denominator = jnp.sum(weights, axis=-1, keepdims=True)
        probabilities = (weights / denominator).astype(jnp.bfloat16)
        mixed_rows = jnp.einsum(
            "hqk,khd->qhd", probabilities, value_heads, preferred_element_type=jnp.float32
        )
        mixed_parts.append(mixed_rows.reshape(block_rows, -1))
        total_parts.append((highest + jnp.log(denominator))[:, :, 0])
    return (jnp.concatenate(mixed_parts, 0).astype(jnp.bfloat16), jnp.concatenate(total_parts, 1))


def attend_back(row_entry):
    head_layout, grad_mixed, log_total, document_starts = row_entry
    query_heads, key_heads, value_heads = split_heads(head_layout)
    length = head_layout.shape[0]
    head_count = query_heads.shape[1]
    grad_heads = grad_mixed.reshape(length, head_count, HEAD)
    block_rows = min(512, length)
    score_scale = HEAD ** (-0.5)
    grad_keys = jnp.zeros(key_heads.shape, jnp.float32)
    grad_values = jnp.zeros(value_heads.shape, jnp.float32)
    query_parts = []
    for offset in range(0, length, block_rows):
        allowed = mask_for(document_starts, offset, block_rows, length)
        query_block = query_heads[offset : offset + block_rows]
        grad_block = grad_heads[offset : offset + block_rows]
        scores = (
            jnp.einsum("qhd,khd->hqk", query_block, key_heads, preferred_element_type=jnp.float32)
            * score_scale
        )
        scores = jnp.where(allowed[None], scores, MASKED)
        probabilities = jnp.exp(scores - log_total[:, offset : offset + block_rows, None])
        grad_probs = jnp.einsum(
            "qhd,khd->hqk", grad_block, value_heads, preferred_element_type=jnp.float32
        )
        inner_sum = jnp.sum(probabilities * grad_probs, axis=-1, keepdims=True)
        grad_scores = (probabilities * (grad_probs - inner_sum)).astype(jnp.bfloat16)
        query_parts.append(
            jnp.einsum("hqk,khd->qhd", grad_scores, key_heads, preferred_element_type=jnp.float32)
            * score_scale
        )
        grad_keys = (
            grad_keys
            + jnp.einsum(
                "hqk,qhd->khd", grad_scores, query_block, preferred_element_type=jnp.float32
            )
            * score_scale
        )
        grad_values = grad_values + jnp.einsum(
            "hqk,qhd->khd",
            probabilities.astype(jnp.bfloat16),
            grad_block,
            preferred_element_type=jnp.float32,
        )
    grad_query = jnp.concatenate(query_parts, 0)
    return jnp.stack(
        [
            grad_query.reshape(length, -1),
            grad_keys.reshape(length, -1),
            grad_values.reshape(length, -1),
        ],
        axis=1,
    ).astype(jnp.bfloat16)


def on_device(
    block_input,
    seg_start,
    ln1_gain,
    ln1_bias,
    qkv_weight,
    query_bias,
    value_bias,
    query_adapter_reduce,
    query_up,
    value_adapter_reduce,
    value_up,
    out_weight,
    out_bias,
    ln2_gain,
    ln2_bias,
    fc_weight,
    fc_bias,
    proj_weight,
    proj_bias,
    grad_out,
):
    groups = block_input.shape[0]
    row_span = block_input.shape[1]
    model_width = block_input.shape[2]
    tokens = groups * row_span
    hidden_units = fc_weight.shape[1]
    row_values = block_input.reshape(tokens, model_width).astype(jnp.float32)
    normed_first, unit_first, inverse_first = norm_forward(row_values, ln1_gain, ln1_bias)
    first_hidden_layer = normed_first.astype(jnp.bfloat16)
    projected = fold_with(
        first_hidden_layer,
        jnp.zeros((tokens, 3 * model_width), jnp.float32),
        lax.all_gather(qkv_weight, "dp", axis=0, tiled=True),
    )
    query_reduce = (
        jnp.dot(first_hidden_layer, query_adapter_reduce, preferred_element_type=jnp.float32)
        * ADAPTER_SCALE
    ).astype(jnp.bfloat16)
    value_reduce = (
        jnp.dot(first_hidden_layer, value_adapter_reduce, preferred_element_type=jnp.float32)
        * ADAPTER_SCALE
    ).astype(jnp.bfloat16)
    split_parts = projected.reshape(tokens, 3, model_width)
    queries = (
        split_parts[:, 0]
        + query_bias
        + jnp.dot(query_reduce, query_up, preferred_element_type=jnp.float32)
    )
    valued = (
        split_parts[:, 2]
        + value_bias
        + jnp.dot(value_reduce, value_up, preferred_element_type=jnp.float32)
    )
    token_layout = jnp.stack([queries, split_parts[:, 1], valued], axis=1).astype(jnp.bfloat16)
    token_layout = token_layout.reshape(groups, row_span, 3, model_width)
    head_layout = lax.all_to_all(token_layout, "seq", split_axis=3, concat_axis=1, tiled=True)
    attended, log_totals = lax.map(attend_row, (head_layout, seg_start))
    mixed_tokens = jax.tree.map(
        lambda part, own: part.astype(own.dtype),
        lax.all_to_all(for_sending(attended), "seq", split_axis=1, concat_axis=2, tiled=True),
        attended,
    ).reshape(tokens, model_width)
    attention_out = fold_with(
        mixed_tokens,
        jnp.zeros((tokens, model_width), jnp.float32),
        lax.all_gather(out_weight, "dp", axis=0, tiled=True),
    )
    middle = row_values + attention_out + out_bias
    normed_second, unit_second, inverse_second = norm_forward(middle, ln2_gain, ln2_bias)
    hidden_second = normed_second.astype(jnp.bfloat16)
    before = (
        fold_with(
            hidden_second,
            jnp.zeros((tokens, hidden_units), jnp.float32),
            lax.all_gather(fc_weight, "dp", axis=0, tiled=True),
        )
        + fc_bias
    )
    gelu_value, gelu_pull = jax.vjp(partial(jax.nn.gelu, approximate=True), before)
    activated = gelu_value.astype(jnp.bfloat16)
    feed_out = fold_with(
        activated,
        jnp.zeros((tokens, model_width), jnp.float32),
        lax.all_gather(proj_weight, "dp", axis=0, tiled=True),
    )
    result_rows = middle + feed_out + proj_bias
    block_output = result_rows.astype(jnp.bfloat16).reshape(groups, row_span, model_width)
    gradient_row_list = grad_out.reshape(tokens, model_width)
    grad_act = map_with(gradient_row_list, lax.all_gather(proj_weight, "dp", axis=0, tiled=True))
    grad_before = gelu_pull(grad_act)[0].astype(jnp.bfloat16)
    grad_second = map_with(grad_before, lax.all_gather(fc_weight, "dp", axis=0, tiled=True))
    grad_middle = gradient_row_list.astype(jnp.float32) + norm_backward(
        grad_second, unit_second, inverse_second, ln2_gain
    )
    grad_attended = grad_middle.astype(jnp.bfloat16)
    grad_mixed = map_with(grad_attended, lax.all_gather(out_weight, "dp", axis=0, tiled=True))
    grad_mixed = grad_mixed.astype(jnp.bfloat16).reshape(groups, row_span, model_width)
    grad_head_layout = lax.all_to_all(grad_mixed, "seq", split_axis=2, concat_axis=1, tiled=True)
    grad_projected = lax.map(attend_back, (head_layout, grad_head_layout, log_totals, seg_start))
    grad_tokens = lax.all_to_all(
        grad_projected, "seq", split_axis=1, concat_axis=3, tiled=True
    ).reshape(tokens, 3 * model_width)
    grad_first = map_with(grad_tokens, lax.all_gather(qkv_weight, "dp", axis=0, tiled=True))
    grad_query = grad_tokens[:, :model_width]
    grad_value = grad_tokens[:, 2 * model_width :]
    gradient_query_reduce = times_transposed(grad_query, query_up).astype(jnp.bfloat16)
    gradient_value_reduce = times_transposed(grad_value, value_up).astype(jnp.bfloat16)
    grad_first = (
        grad_first
        + (
            times_transposed(gradient_query_reduce, query_adapter_reduce)
            + times_transposed(gradient_value_reduce, value_adapter_reduce)
        )
        * ADAPTER_SCALE
    )
    grad_input = grad_middle + norm_backward(grad_first, unit_first, inverse_first, ln1_gain)
    shard_query_reduce = (
        across_token_rows(first_hidden_layer, gradient_query_reduce) * ADAPTER_SCALE
    )
    local_query_up = across_token_rows(query_reduce, grad_query)
    shard_value_reduce = (
        across_token_rows(first_hidden_layer, gradient_value_reduce) * ADAPTER_SCALE
    )
    local_value_up = across_token_rows(value_reduce, grad_value)
    summed = lax.psum(
        (shard_query_reduce, local_query_up, shard_value_reduce, local_value_up), ("dp", "seq")
    )
    return (
        block_output,
        grad_input.reshape(groups, row_span, model_width),
        summed[0],
        summed[1],
        summed[2],
        summed[3],
    )


def solution(mesh):
    return jax.shard_map(
        on_device,
        mesh=mesh,
        in_specs=(
            P("dp", "seq", None),
            P("dp", None),
            P(),
            P(),
            P("dp", None),
            P(),
            P(),
            P(),
            P(),
            P(),
            P(),
            P("dp", None),
            P(),
            P(),
            P(),
            P("dp", None),
            P(),
            P("dp", None),
            P(),
            P("dp", "seq", None),
        ),
        out_specs=(P("dp", "seq", None), P("dp", "seq", None), P(), P(), P(), P()),
        check_vma=False,
    )
```

profile of v0, /device:TPU:1, one launch (start us, length us, event | category | flops | bytes accessed | tf_op | source)
XLA Modules:
  0.0 919.3 jit_solution(9611403195169453674)
XLA Ops:
  14.8 43.2 %all-gather.5.cloned.1.call-done = bf16[1024,3072]{1,0:T(8,128)(2,1)} async-done(((bf16[128,3072]{1,0:T(8,128)(2,1)}), bf16[1024,3072]{1,0:T(8,128)(2,1)}) %all-gather.5.cloned.1.call-update) | async-done | bytes 6291472 | tf_op jit(solution)/shard_map/all_gather | solution.py:195
  58.0 8.6 copy.34
  66.6 7.4 fusion.118
  78.7 3.0 copy.37
  81.6 4.1 copy.36
  85.8 3.7 fusion.56
  89.5 4.2 copy.35
  93.6 8.3 pad_maximum_fusion.1
  102.0 5.2 all-to-all-start
  107.8 137.4 %all-to-all-done = bf16[3,256,3,1024]{1,0,2,3:T(4,128)(2,1)} async-done(((bf16[3,256,3,1024]{1,0,2,3:T(4,128)(2,1)}), bf16[3,256,3,1024]{1,0,2,3:T(4,128)(2,1)}, u32[]{:S(2)}, u32[]{:S(2)}) %all-to-all-start) | async-done | bytes 4718624 | tf_op jit(solution)/shard_map/all_to_all | solution.py:218
  245.2 9.4 %copy.38 = bf16[3,4,256,3,256]{2,1,4,3,0:T(4,128)(2,1)} copy(bf16[3,4,256,3,256]{2,0,3,4,1:T(4,128)(2,1)} %bitcast.40) | data formatting | bytes 9437184 | tf_op jit(solution)/shard_map/all_to_all | solution.py:218
  254.6 8.7 all_to_all.51
  263.3 51.6 %while.22 = (s32[]{:T(128)}, bf16[3,1024,256]{1,2,0:T(8,128)(2,1)S(1)}, f32[3,4,1024]{2,1,0:T(4,128)S(1)}, bf16[3,1024,3,256]{1,3,2,0:T(8,128)(2,1)}, s32[3,1024]{1,0:T(4,128)S(1)}, /*index=5*/s32[]{:T(128)}, s32[]{:T(128)}, s32[]{}) while((s32[]{:T(128)}, bf16[3,1024,256]{1,2,0:T(8,128)(2,1)S(1)}, f32[3,4,1024]{2,1,0:T(4,128)S(1)}, ...), condition=%wide.region_7.8_spmd, body=%wide.region_2.7_spmd.sunk | while | flops 1128530432 | bytes 65192060 | solution.py:219
  267.7 2.4 fusion.241
  270.1 3.1 fusion.242
  274.9 2.4 fusion.237
  277.3 3.1 fusion.238
  284.9 2.4 fusion.241
  287.3 3.1 fusion.242
  292.1 2.4 fusion.237
  294.6 3.1 fusion.238
  302.1 2.4 fusion.241
  304.6 3.1 fusion.242
  309.4 2.4 fusion.237
  311.8 3.1 fusion.238
  316.1 2.9 copy.39
  319.1 49.9 %all_to_all.66 = bf16[3,1024,256]{2,0,1:T(4,128)(2,1)S(1)} all-to-all(bf16[3,1024,256]{2,0,1:T(4,128)(2,1)S(1)} %copy.39), channel_id=1, replica_groups=mesh['dp'=8,'seq'=4] {'seq'}, dimensions={1} | all-to-all | bytes 3145728 | tf_op jit(solution)/shard_map/all_to_all | solution.py:222
  370.9 3.6 fusion.112
  376.7 13.8 %fusion.74 = f32[768,4096]{1,0:T(8,128)} fusion(bf16[1024,4096]{1,0:T(8,128)(2,1)} %all-gather.9.cloned.1.call-done, f32[768,1024]{1,0:T(8,128)} %copy-done.6, f32[1024]{0:T(1024)S(1)} %copy-done.38, f32[1024]{0:T(1024)S(1)} %copy-done.31, f32[768]{0:T(1024)S(1)} %add_rsqrt_fusion, f32[768]{0:T(1024)S(1)} %broadcast_multiply_fusion.4), kind=kOutput, calls=%fused_computation.126 | convolution fusion | flops 6446383104 | bytes 24131584 | tf_op jit(solution)/shard_map/dot_general | solution.py:40
  390.5 27.4 %multiply_reduce_fusion.4 = (f32[768]{0:T(1024)S(1)}, f32[768]{0:T(1024)S(1)}, f32[768,1024]{1,0:T(8,128)}) fusion(f32[1024]{0:T(1024)S(1)} %copy-done.31, f32[768]{0:T(1024)S(1)} %add_rsqrt_fusion, f32[768,1024]{1,0:T(8,128)S(1)} %copy-done.7, f32[768]{0:T(1024)S(1)} %broadcast_multiply_fusion.4, bf16[1024,4096]{1,0:T(8,128)(2,1)} %all-gather.9.cloned.1.call-done, ...), kind=kOutput, calls=%fused_computation.124 | convolution fusion | flops 12955678720 | bytes 37257216 | tf_op jit(solution)/shard_map/dot_general | solution.py:44
  418.0 3.1 multiply_add_fusion
  422.9 2.6 copy.41
  425.5 3.6 all-to-all-start.2
  429.2 47.6 %all-to-all-done.2 = bf16[3,256,1024]{1,0,2:T(4,128)(2,1)S(1)} async-done(((bf16[3,256,1024]{1,0,2:T(4,128)(2,1)}), bf16[3,256,1024]{1,0,2:T(4,128)(2,1)S(1)}, u32[]{:S(2)}, u32[]{:S(2)}) %all-to-all-start.2) | async-done | bytes 1572896 | tf_op jit(solution)/shard_map/all_to_all | solution.py:260
  476.8 2.6 copy.42
  479.4 2.8 all_to_all.58
  482.3 106.2 %while.23 = (s32[]{:T(128)}, bf16[3,1024,3,256]{1,3,2,0:T(8,128)(2,1)}, bf16[3,1024,3,256]{1,3,2,0:T(8,128)(2,1)}, s32[3,1024]{1,0:T(4,128)S(1)}, f32[3,4,1024]{...) while((s32[]{:T(128)}, bf16[3,1024,3,256]{1,3,2,0:T(8,128)(2,1)}, ...), condition=%wide.region_15.16_spmd, body=%wide.region_12.15_spmd.sunk | while | flops 2758013440 | bytes 152731792 | solution.py:261
  487.7 2.4 fusion.269
  490.1 2.5 fusion.272
  492.6 5.4 multiply_reduce_fusion.8
  498.0 5.5 multiply_reduce_fusion.7
  503.5 8.3 multiply_convert_fusion.7
  523.0 2.4 fusion.269
  525.4 2.5 fusion.272
  527.9 5.4 multiply_reduce_fusion.8
  533.3 5.5 multiply_reduce_fusion.7
  538.8 8.3 multiply_convert_fusion.7
  558.3 2.4 fusion.269
  560.7 2.5 fusion.272
  563.2 5.4 multiply_reduce_fusion.8
  568.6 5.5 multiply_reduce_fusion.7
  574.1 8.3 multiply_convert_fusion.7
  588.5 10.3 %copy.43 = bf16[3,1024,3,256]{3,2,0,1:T(4,128)(2,1)} copy(bf16[3,1024,3,256]{1,3,2,0:T(8,128)(2,1)} %get-tuple-element.68) | data formatting | bytes 9437184 | tf_op jit(solution)/shard_map/while | solution.py:261
  598.8 5.5 all-to-all-start.3
  604.4 14.5 %add_convert_fusion = bf16[768,1024]{1,0:T(8,128)(2,1)} fusion(f32[768,1024]{1,0:T(8,128)S(1)} %copy-done.8, bf16[4096,1024]{1,0:T(8,128)(2,1)} %all-gather.11.cloned.1.call-done, f32[768,4096]{1,0:T(8,128)} %fusion.74, f32[4096]{0:T(1024)S(1)} %copy-done.36, f32[1024]{0:T(1024)S(1)} %copy-done.39), kind=kOutput, calls=%fused_computation.120 | convolution fusion | flops 6476267520 | bytes 25710592 | tf_op jit(solution)/shard_map/dot_general | solution.py:40
  618.8 123.1 %all-to-all-done.3 = bf16[3,1024,3,256]{3,2,0,1:T(4,128)(2,1)} async-done(((bf16[3,1024,3,256]{3,2,0,1:T(4,128)(2,1)}), bf16[3,1024,3,256]{3,2,0,1:T(4,128)(2,1)}, u32[]{:S(2)}, u32[]{:S(2)}) %all-to-all-start.3) | async-done | bytes 4718624 | tf_op jit(solution)/shard_map/all_to_all | solution.py:262
  741.9 11.0 %copy.47 = bf16[3,4,256,3,256]{4,1,3,2,0:T(4,128)(2,1)} copy(bf16[3,4,256,3,256]{4,3,0,2,1:T(4,128)(2,1)} %bitcast.48) | data formatting | bytes 9437184 | tf_op jit(solution)/shard_map/all_to_all | solution.py:262
  753.0 9.6 %reshape.412 = bf16[768,3072]{1,0:T(8,128)(2,1)} reshape(bf16[3,256,3,4,256]{4,3,2,1,0:T(4,128)(2,1)} %bitcast.288) | data formatting | bytes 9437184 | tf_op jit(solution)/shard_map/reshape | solution.py:264
  766.5 2.4 fusion.84
  768.9 2.3 fusion.80
  775.4 8.7 fusion.119
  784.2 2.9 fusion.106
  787.1 5.4 fusion.72
  792.5 114.5 %all-reduce.3.cloned.1.call-done = (f32[1024,4]{0,1:T(4,128)}, f32[4,1024]{1,0:T(4,128)}, f32[1024,4]{0,1:T(4,128)}, f32[4,1024]{1,0:T(4,128)}) async-done(((f32[1024,4]{0,1:T(4,128)}, f32[4,1024]{1,0:T(4,128)}, f32[1024,4]{0,1:T(4,128)}, f32[4,1024]{1,0:T(4,128)}), (f32[1024,4]{0,1:T(4,128)}, f32[4,1024]{1,0:T(4,128)}, f32[1024,4]{0,1:T(4,128)}, f32[4,1024]{1,0:T(4,128)})) %all-reduce.3.cloned.1.call-update) | async-done | bytes 65552 | tf_op jit(solution)/shard_map/psum | solution.py:287
  (216 shorter events, 84.6 us)
Async XLA Ops:
  7.2 5.3 copy-start
  7.2 4.0 copy-start.1
  7.2 4.6 copy-start.22
  7.2 4.6 copy-start.26
  7.2 50.8 %all-gather.5.cloned.1.call-start = ((), (), s32[]{:S(2)}) async-start(), calls=%async_computation.4 | async-start | bytes 7077888 | tf_op jit(solution)/shard_map/all_gather | solution.py:195
  7.9 362.9 %all-gather.7.cloned.1.call-start = ((), (), s32[]{:S(2)}) async-start(), calls=%async_computation.5 | async-start | bytes 2359296 | tf_op jit(solution)/shard_map/all_gather | solution.py:228
  8.7 368.0 %all-gather.9.cloned.1.call-start = ((), (), s32[]{:S(2)}) async-start(), calls=%async_computation.6 | async-start | bytes 9437184 | tf_op jit(solution)/shard_map/all_gather | solution.py:237
  9.4 4.2 copy-start.24
  11.2 1.8 copy-start.14
  11.8 1.2 copy-start.16
  12.4 1.2 copy-start.4
  13.6 62.0 %copy-start.18 = (bf16[768,4]{0,1:T(4,128)(2,1)}, bf16[768,4]{0,1:T(4,128)(2,1)S(1)}, u32[]{:S(2)}) copy-start(bf16[768,4]{0,1:T(4,128)(2,1)S(1)} %fusion.89) | copy-start | bytes 18436
  14.1 71.6 %copy-start.20 = (bf16[768,4]{0,1:T(4,128)(2,1)}, bf16[768,4]{0,1:T(4,128)(2,1)S(1)}, u32[]{:S(2)}) copy-start(bf16[768,4]{0,1:T(4,128)(2,1)S(1)} %fusion.88) | copy-start | bytes 18436
  66.6 9.0 copy-start.27
  66.6 9.0 copy-start.32
  74.0 4.6 copy-start.11
  78.7 7.1 copy-start.29
  78.7 7.1 copy-start.33
  102.0 143.3 %all-to-all-start = ((bf16[3,256,3,1024]{1,0,2,3:T(4,128)(2,1)}), bf16[3,256,3,1024]{1,0,2,3:T(4,128)(2,1)}, u32[]{:S(2)}, u32[]{:S(2)}) async-start(bf16[3,256,3,1024]{1,0,2,3:T(4,128)(2,1)} %pad_maximum_fusion.1), calls=%async_computation | async-start | bytes 12582912 | tf_op jit(solution)/shard_map/all_to_all | solution.py:218
  107.2 283.3 %all-gather.11.cloned.1.call-start = ((), (), s32[]{:S(2)}) async-start(), calls=%async_computation.7 | async-start | bytes 9437184 | tf_op jit(solution)/shard_map/all_gather | solution.py:246
  254.6 8.7 copy-start.13
  315.0 1.1 copy-start.12
  369.0 1.9 copy-start.2
  369.0 1.9 copy-start.37
  370.9 5.8 copy-start.31
  370.9 5.8 copy-start.38
  374.5 1.7 copy-start.6
  376.6 13.9 %copy-start.7 = (f32[768,1024]{1,0:T(8,128)S(1)}, f32[768,1024]{1,0:T(8,128)}, u32[]{:S(2)}) copy-start(f32[768,1024]{1,0:T(8,128)} %copy-done.6) | copy-start | bytes 9437188
  376.6 13.9 %copy-start.35 = (f32[4096]{0:T(1024)S(1)}, f32[4096]{0:T(1024)}, u32[]{:S(2)}) copy-start(f32[4096]{0:T(1024)} %param.40) | copy-start | bytes 49156
  418.0 3.1 copy-start.34
  421.1 1.8 copy-start.9
  425.5 51.3 %all-to-all-start.2 = ((bf16[3,256,1024]{1,0,2:T(4,128)(2,1)}), bf16[3,256,1024]{1,0,2:T(4,128)(2,1)S(1)}, u32[]{:S(2)}, u32[]{:S(2)}) async-start(bf16[3,256,1024]{1,0,2:T(4,128)(2,1)} %copy.41), calls=%async_computation.2 | async-start | bytes 4194304 | tf_op jit(solution)/shard_map/all_to_all | solution.py:260
  598.8 5.6 copy-start.8
  598.8 5.6 copy-start.36
  598.8 5.6 copy-start.39
  598.8 143.1 %all-to-all-start.3 = ((bf16[3,1024,3,256]{3,2,0,1:T(4,128)(2,1)}), bf16[3,1024,3,256]{3,2,0,1:T(4,128)(2,1)}, u32[]{:S(2)}, u32[]{:S(2)}) async-start(bf16[3,1024,3,256]{3,2,0,1:T(4,128)(2,1)} %copy.43), calls=%async_computation.3 | async-start | bytes 12582912 | tf_op jit(solution)/shard_map/all_to_all | solution.py:262
  604.3 302.7 %all-reduce.3.cloned.1.call-start = ((), (), s32[]{:S(2)}) async-start(), calls=%async_computation.8 | async-start | bytes 131072 | tf_op jit(solution)/shard_map/psum | solution.py:287
  753.0 9.6 %copy-start.28 = (bf16[4,1024]{1,0:T(4,128)(2,1)S(1)}, bf16[4,1024]{1,0:T(4,128)(2,1)}, u32[]{:S(2)}) copy-start(bf16[4,1024]{1,0:T(4,128)(2,1)} %param.34) | copy-start | bytes 24580
  753.0 11.7 %copy-start.30 = (bf16[4,1024]{1,0:T(4,128)(2,1)S(1)}, bf16[4,1024]{1,0:T(4,128)(2,1)}, u32[]{:S(2)}) copy-start(bf16[4,1024]{1,0:T(4,128)(2,1)} %param.32) | copy-start | bytes 24580
  753.0 13.6 %copy-start.21 = (bf16[768,4]{0,1:T(4,128)(2,1)S(1)}, bf16[768,4]{0,1:T(4,128)(2,1)}, u32[]{:S(2)}) copy-start(bf16[768,4]{0,1:T(4,128)(2,1)} %copy-done.20) | copy-start | bytes 18436
  762.5 6.4 copy-start.19
  762.6 8.7 copy-start.5
  762.6 9.6 %copy-start.25 = (bf16[1024,4]{0,1:T(4,128)(2,1)S(1)}, bf16[1024,4]{0,1:T(4,128)(2,1)}, u32[]{:S(2)}) copy-start(bf16[1024,4]{0,1:T(4,128)(2,1)} %param.31) | copy-start | bytes 24580
  775.4 8.8 copy-start.3
  775.4 8.8 copy-start.10
  775.4 8.8 copy-start.15
  775.4 8.8 copy-start.17
  775.4 8.8 copy-start.23
Sparse Core Ops, SparseCore 0:
  9.9 48.0 all-gather.4
  59.9 27.8 all-gather.6
  89.7 54.3 all-gather.8
  145.9 54.3 all-gather.10
  787.2 119.7 all-reduce.2
where the time goes:
time: 928 us; the launch traced here: 919 us
  waiting for transfers between devices  468 us (50%)
  matrix products  197 us (21%)
  local copies, waits for them, and re-layouts  103 us (11%)
  other arithmetic  70.1 us (8%)
  blocking collectives  49.9 us (5%)
  between operations  14.8 us (2%)
  starting transfers between devices  14.7 us (2%)
    all_to_all x1, waiting for transfers between devices, on_device(): lax.all_to_all(token_layout, 'seq', split_axis=3, concat_axis=1, tiled=True)  137 us
    all_to_all x1, waiting for transfers between devices, on_device(): lax.all_to_all(grad_projected, 'seq', split_axis=1, concat_axis=3, tiled=...  123 us
    psum x1, waiting for transfers between devices, on_device(): lax.psum((shard_query_reduce, local_query_up, shard_value_reduce, local_v...  114 us
    all_to_all x1, blocking collectives, on_device(): lax.all_to_all(for_sending(attended), 'seq', split_axis=1, concat_axis=2,...  49.9 us
    all_to_all x1, waiting for transfers between devices, on_device(): lax.all_to_all(grad_mixed, 'seq', split_axis=2, concat_axis=1, tiled=True)  47.6 us
    dot_general x7, matrix products, times_transposed(): lax.dot_general(left_side, right_side, (((1,), (1,)), ((), ())), preferre...  47.1 us
    all_gather x1, waiting for transfers between devices, on_device(): lax.all_gather(qkv_weight, 'dp', axis=0, tiled=True)  43.2 us
    dot_general x4, matrix products, fold_with(): jnp.dot(columns, weight_piece, preferred_element_type=jnp.float32)  39.2 us
  transfers between devices with their start and end apart: 8, of which 5 were waited for; matrix products, arithmetic and copies ran while one was open for 16% of the time, Pallas kernels for 0%

commit v1 on v0

--- a/solution.py
+++ b/solution.py
@@ -284,9 +284,8 @@
         across_token_rows(first_hidden_layer, gradient_value_reduce) * ADAPTER_SCALE
     )
     local_value_up = across_token_rows(value_reduce, grad_value)
-    summed = lax.psum(
-        (shard_query_reduce, local_query_up, shard_value_reduce, local_value_up), ("dp", "seq")
-    )
+    half = lax.psum((shard_query_reduce, local_query_up, shard_value_reduce, local_value_up), "seq")
+    summed = lax.psum(half, "dp")
     return (
         block_output,
         grad_input.reshape(groups, row_span, model_width),

time: 928 us -> 899 us (0.969)
  waiting for transfers between devices: 468 us -> 437 us
    psum x1, waiting for transfers between devices: 114 us -> 31.1 us  [on_device(): lax.psum((shard_query_reduce, local_query_up, shard_value_reduce, local_v...]
    psum x0 -> x1, waiting for transfers between devices: none -> 52.3 us  [on_device(): summed = lax.psum(half, 'dp')]
  transfers between devices with their start and end apart: 8 -> 9, of which waited for: 5 -> 6; matrix products, arithmetic and copies ran while one was open for 16% -> 17% of each run, Pallas kernels for 0% -> 0%
where the time goes in v1:
time: 899 us; the launch traced here: 889 us
  waiting for transfers between devices  437 us (49%)
  matrix products  197 us (22%)
  local copies, waits for them, and re-layouts  103 us (11%)
  other arithmetic  70.1 us (8%)
  blocking collectives  49.9 us (6%)
  between operations  15.1 us (2%)
  starting transfers between devices  14.8 us (2%)
    all_to_all x1, waiting for transfers between devices, on_device(): lax.all_to_all(token_layout, 'seq', split_axis=3, concat_axis=1, tiled=True)  137 us
    all_to_all x1, waiting for transfers between devices, on_device(): lax.all_to_all(grad_projected, 'seq', split_axis=1, concat_axis=3, tiled=...  123 us
    psum x1, waiting for transfers between devices, on_device(): summed = lax.psum(half, 'dp')  52.3 us
    all_to_all x1, blocking collectives, on_device(): lax.all_to_all(for_sending(attended), 'seq', split_axis=1, concat_axis=2,...  49.9 us
    all_to_all x1, waiting for transfers between devices, on_device(): lax.all_to_all(grad_mixed, 'seq', split_axis=2, concat_axis=1, tiled=True)  47.6 us
    dot_general x7, matrix products, times_transposed(): lax.dot_general(left_side, right_side, (((1,), (1,)), ((), ())), preferre...  47.2 us
    all_gather x1, waiting for transfers between devices, on_device(): lax.all_gather(qkv_weight, 'dp', axis=0, tiled=True)  43.2 us
    dot_general x4, matrix products, fold_with(): jnp.dot(columns, weight_piece, preferred_element_type=jnp.float32)  39.2 us
  transfers between devices with their start and end apart: 9, of which 6 were waited for; matrix products, arithmetic and copies ran while one was open for 17% of the time, Pallas kernels for 0%

profile of v1, /device:TPU:1, one launch (start us, length us, event | category | flops | bytes accessed | tf_op | source)
XLA Modules:
  0.0 888.7 jit_solution(8683328753034579786)
XLA Ops:
  14.8 43.2 %all-gather.5.cloned.1.call-done = bf16[1024,3072]{1,0:T(8,128)(2,1)} async-done(((bf16[128,3072]{1,0:T(8,128)(2,1)}), bf16[1024,3072]{1,0:T(8,128)(2,1)}) %all-gather.5.cloned.1.call-update) | async-done | bytes 6291472 | tf_op jit(solution)/shard_map/all_gather | solution.py:195
  58.0 8.7 copy.34
  66.7 7.4 fusion.118
  78.7 3.0 copy.37
  81.6 4.1 copy.36
  85.8 3.7 fusion.56
  89.5 4.2 copy.35
  93.6 8.3 pad_maximum_fusion.1
  102.0 5.2 all-to-all-start
  107.8 137.4 %all-to-all-done = bf16[3,256,3,1024]{1,0,2,3:T(4,128)(2,1)} async-done(((bf16[3,256,3,1024]{1,0,2,3:T(4,128)(2,1)}), bf16[3,256,3,1024]{1,0,2,3:T(4,128)(2,1)}, u32[]{:S(2)}, u32[]{:S(2)}) %all-to-all-start) | async-done | bytes 4718624 | tf_op jit(solution)/shard_map/all_to_all | solution.py:218
  245.2 9.4 %copy.38 = bf16[3,4,256,3,256]{2,1,4,3,0:T(4,128)(2,1)} copy(bf16[3,4,256,3,256]{2,0,3,4,1:T(4,128)(2,1)} %bitcast.40) | data formatting | bytes 9437184 | tf_op jit(solution)/shard_map/all_to_all | solution.py:218
  254.6 8.7 all_to_all.51
  263.4 51.6 %while.22 = (s32[]{:T(128)}, bf16[3,1024,256]{1,2,0:T(8,128)(2,1)S(1)}, f32[3,4,1024]{2,1,0:T(4,128)S(1)}, bf16[3,1024,3,256]{1,3,2,0:T(8,128)(2,1)}, s32[3,1024]{1,0:T(4,128)S(1)}, /*index=5*/s32[]{:T(128)}, s32[]{:T(128)}, s32[]{}) while((s32[]{:T(128)}, bf16[3,1024,256]{1,2,0:T(8,128)(2,1)S(1)}, f32[3,4,1024]{2,1,0:T(4,128)S(1)}, ...), condition=%wide.region_7.8_spmd, body=%wide.region_2.7_spmd.sunk | while | flops 1128530432 | bytes 65192060 | solution.py:219
  267.7 2.4 fusion.241
  270.1 3.1 fusion.242
  274.9 2.4 fusion.237
  277.3 3.1 fusion.238
  284.9 2.4 fusion.241
  287.3 3.1 fusion.242
  292.1 2.4 fusion.237
  294.6 3.1 fusion.238
  302.1 2.4 fusion.241
  304.6 3.1 fusion.242
  309.4 2.4 fusion.237
  311.8 3.1 fusion.238
  316.2 2.9 copy.39
  319.1 49.9 %all_to_all.66 = bf16[3,1024,256]{2,0,1:T(4,128)(2,1)S(1)} all-to-all(bf16[3,1024,256]{2,0,1:T(4,128)(2,1)S(1)} %copy.39), channel_id=1, replica_groups=mesh['dp'=8,'seq'=4] {'seq'}, dimensions={1} | all-to-all | bytes 3145728 | tf_op jit(solution)/shard_map/all_to_all | solution.py:222
  370.9 3.6 fusion.112
  376.7 13.8 %fusion.74 = f32[768,4096]{1,0:T(8,128)} fusion(bf16[1024,4096]{1,0:T(8,128)(2,1)} %all-gather.9.cloned.1.call-done, f32[768,1024]{1,0:T(8,128)} %copy-done.6, f32[1024]{0:T(1024)S(1)} %copy-done.38, f32[1024]{0:T(1024)S(1)} %copy-done.31, f32[768]{0:T(1024)S(1)} %add_rsqrt_fusion, f32[768]{0:T(1024)S(1)} %broadcast_multiply_fusion.4), kind=kOutput, calls=%fused_computation.126 | convolution fusion | flops 6446383104 | bytes 24131584 | tf_op jit(solution)/shard_map/dot_general | solution.py:40
  390.6 27.5 %multiply_reduce_fusion.4 = (f32[768]{0:T(1024)S(1)}, f32[768]{0:T(1024)S(1)}, f32[768,1024]{1,0:T(8,128)}) fusion(f32[1024]{0:T(1024)S(1)} %copy-done.31, f32[768]{0:T(1024)S(1)} %add_rsqrt_fusion, f32[768,1024]{1,0:T(8,128)S(1)} %copy-done.7, f32[768]{0:T(1024)S(1)} %broadcast_multiply_fusion.4, bf16[1024,4096]{1,0:T(8,128)(2,1)} %all-gather.9.cloned.1.call-done, ...), kind=kOutput, calls=%fused_computation.124 | convolution fusion | flops 12955678720 | bytes 37257216 | tf_op jit(solution)/shard_map/dot_general | solution.py:44
  418.0 3.1 multiply_add_fusion
  423.0 2.6 copy.41
  425.6 3.6 all-to-all-start.2
  429.2 47.6 %all-to-all-done.2 = bf16[3,256,1024]{1,0,2:T(4,128)(2,1)S(1)} async-done(((bf16[3,256,1024]{1,0,2:T(4,128)(2,1)}), bf16[3,256,1024]{1,0,2:T(4,128)(2,1)S(1)}, u32[]{:S(2)}, u32[]{:S(2)}) %all-to-all-start.2) | async-done | bytes 1572896 | tf_op jit(solution)/shard_map/all_to_all | solution.py:260
  476.9 2.6 copy.42
  479.5 2.8 all_to_all.58
  482.3 106.3 %while.23 = (s32[]{:T(128)}, bf16[3,1024,3,256]{1,3,2,0:T(8,128)(2,1)}, bf16[3,1024,3,256]{1,3,2,0:T(8,128)(2,1)}, s32[3,1024]{1,0:T(4,128)S(1)}, f32[3,4,1024]{...) while((s32[]{:T(128)}, bf16[3,1024,3,256]{1,3,2,0:T(8,128)(2,1)}, ...), condition=%wide.region_15.16_spmd, body=%wide.region_12.15_spmd.sunk | while | flops 2758013440 | bytes 152731792 | solution.py:261
  487.8 2.4 fusion.269
  490.2 2.5 fusion.272
  492.7 5.4 multiply_reduce_fusion.8
  498.1 5.5 multiply_reduce_fusion.7
  503.6 8.3 multiply_convert_fusion.7
  523.1 2.4 fusion.269
  525.6 2.5 fusion.272
  528.0 5.4 multiply_reduce_fusion.8
  533.4 5.5 multiply_reduce_fusion.7
  538.9 8.3 multiply_convert_fusion.7
  558.4 2.4 fusion.269
  560.9 2.5 fusion.272
  563.4 5.4 multiply_reduce_fusion.8
  568.8 5.5 multiply_reduce_fusion.7
  574.3 8.3 multiply_convert_fusion.7
  588.6 10.2 %copy.43 = bf16[3,1024,3,256]{3,2,0,1:T(4,128)(2,1)} copy(bf16[3,1024,3,256]{1,3,2,0:T(8,128)(2,1)} %get-tuple-element.68) | data formatting | bytes 9437184 | tf_op jit(solution)/shard_map/while | solution.py:261
  598.9 5.5 all-to-all-start.3
  604.5 14.5 %add_convert_fusion = bf16[768,1024]{1,0:T(8,128)(2,1)} fusion(f32[768,1024]{1,0:T(8,128)S(1)} %copy-done.8, bf16[4096,1024]{1,0:T(8,128)(2,1)} %all-gather.11.cloned.1.call-done, f32[768,4096]{1,0:T(8,128)} %fusion.74, f32[4096]{0:T(1024)S(1)} %copy-done.36, f32[1024]{0:T(1024)S(1)} %copy-done.39), kind=kOutput, calls=%fused_computation.120 | convolution fusion | flops 6476267520 | bytes 25710592 | tf_op jit(solution)/shard_map/dot_general | solution.py:40
  618.9 123.1 %all-to-all-done.3 = bf16[3,1024,3,256]{3,2,0,1:T(4,128)(2,1)} async-done(((bf16[3,1024,3,256]{3,2,0,1:T(4,128)(2,1)}), bf16[3,1024,3,256]{3,2,0,1:T(4,128)(2,1)}, u32[]{:S(2)}, u32[]{:S(2)}) %all-to-all-start.3) | async-done | bytes 4718624 | tf_op jit(solution)/shard_map/all_to_all | solution.py:262
  742.0 11.1 %copy.47 = bf16[3,4,256,3,256]{4,1,3,2,0:T(4,128)(2,1)} copy(bf16[3,4,256,3,256]{4,3,0,2,1:T(4,128)(2,1)} %bitcast.48) | data formatting | bytes 9437184 | tf_op jit(solution)/shard_map/all_to_all | solution.py:262
  753.1 9.6 %reshape.412 = bf16[768,3072]{1,0:T(8,128)(2,1)} reshape(bf16[3,256,3,4,256]{4,3,2,1,0:T(4,128)(2,1)} %bitcast.288) | data formatting | bytes 9437184 | tf_op jit(solution)/shard_map/reshape | solution.py:264
  766.6 2.4 fusion.84
  775.5 8.7 fusion.119
  784.3 2.9 fusion.106
  787.3 31.1 %all-reduce.7.cloned.1.call-done = (f32[1024,4]{0,1:T(4,128)}, f32[4,1024]{1,0:T(4,128)}, f32[1024,4]{0,1:T(4,128)}, f32[4,1024]{1,0:T(4,128)}) async-done(((f32[1024,4]{0,1:T(4,128)}, f32[4,1024]{1,0:T(4,128)}, f32[1024,4]{0,1:T(4,128)}, f32[4,1024]{1,0:T(4,128)}), (f32[1024,4]{0,1:T(4,128)}, f32[4,1024]{1,0:T(4,128)}, f32[1024,4]{0,1:T(4,128)}, f32[4,1024]{1,0:T(4,128)})) %all-reduce.7.cloned.1.call-update) | async-done | bytes 65552 | tf_op jit(solution)/shard_map/psum | solution.py:287
  818.4 5.4 fusion.72
  823.9 52.3 %all-reduce.5.cloned.1.call-done = (f32[1024,4]{0,1:T(4,128)}, f32[4,1024]{1,0:T(4,128)}, f32[1024,4]{0,1:T(4,128)}, f32[4,1024]{1,0:T(4,128)}) async-done(((f32[1024,4]{0,1:T(4,128)}, f32[4,1024]{1,0:T(4,128)}, f32[1024,4]{0,1:T(4,128)}, f32[4,1024]{1,0:T(4,128)}), (f32[1024,4]{0,1:T(4,128)}, f32[4,1024]{1,0:T(4,128)}, f32[1024,4]{0,1:T(4,128)}, f32[4,1024]{1,0:T(4,128)})) %all-reduce.5.cloned.1.call-update) | async-done | bytes 65552 | tf_op jit(solution)/shard_map/psum | solution.py:288
  (219 shorter events, 87.0 us)
Async XLA Ops:
  7.2 5.3 copy-start
  7.2 4.0 copy-start.1
  7.2 4.6 copy-start.22
  7.2 4.6 copy-start.26
  7.2 50.8 %all-gather.5.cloned.1.call-start = ((), (), s32[]{:S(2)}) async-start(), calls=%async_computation.4 | async-start | bytes 7077888 | tf_op jit(solution)/shard_map/all_gather | solution.py:195
  7.9 362.9 %all-gather.7.cloned.1.call-start = ((), (), s32[]{:S(2)}) async-start(), calls=%async_computation.5 | async-start | bytes 2359296 | tf_op jit(solution)/shard_map/all_gather | solution.py:228
  8.7 368.0 %all-gather.9.cloned.1.call-start = ((), (), s32[]{:S(2)}) async-start(), calls=%async_computation.6 | async-start | bytes 9437184 | tf_op jit(solution)/shard_map/all_gather | solution.py:237
  9.4 4.2 copy-start.24
  11.2 1.8 copy-start.14
  11.8 1.2 copy-start.16
  12.4 1.2 copy-start.4
  13.6 62.1 %copy-start.18 = (bf16[768,4]{0,1:T(4,128)(2,1)}, bf16[768,4]{0,1:T(4,128)(2,1)S(1)}, u32[]{:S(2)}) copy-start(bf16[768,4]{0,1:T(4,128)(2,1)S(1)} %fusion.89) | copy-start | bytes 18436
  14.1 71.7 %copy-start.20 = (bf16[768,4]{0,1:T(4,128)(2,1)}, bf16[768,4]{0,1:T(4,128)(2,1)S(1)}, u32[]{:S(2)}) copy-start(bf16[768,4]{0,1:T(4,128)(2,1)S(1)} %fusion.88) | copy-start | bytes 18436
  66.7 9.0 %copy-start.27 = (bf16[4,1024]{1,0:T(4,128)(2,1)S(1)}, bf16[4,1024]{1,0:T(4,128)(2,1)}, u32[]{:S(2)}) copy-start(bf16[4,1024]{1,0:T(4,128)(2,1)} %param.34) | copy-start | bytes 24580
  66.7 9.0 %copy-start.32 = (f32[1024]{0:T(1024)S(1)}, f32[1024]{0:T(1024)}, u32[]{:S(2)}) copy-start(f32[1024]{0:T(1024)} %param.30) | copy-start | bytes 12292
  74.0 4.6 copy-start.11
  78.7 7.1 copy-start.29
  78.7 7.1 copy-start.33
  102.0 143.3 %all-to-all-start = ((bf16[3,256,3,1024]{1,0,2,3:T(4,128)(2,1)}), bf16[3,256,3,1024]{1,0,2,3:T(4,128)(2,1)}, u32[]{:S(2)}, u32[]{:S(2)}) async-start(bf16[3,256,3,1024]{1,0,2,3:T(4,128)(2,1)} %pad_maximum_fusion.1), calls=%async_computation | async-start | bytes 12582912 | tf_op jit(solution)/shard_map/all_to_all | solution.py:218
  107.2 283.3 %all-gather.11.cloned.1.call-start = ((), (), s32[]{:S(2)}) async-start(), calls=%async_computation.7 | async-start | bytes 9437184 | tf_op jit(solution)/shard_map/all_gather | solution.py:246
  254.6 8.7 copy-start.13
  315.0 1.1 copy-start.12
  369.0 1.9 copy-start.2
  369.0 1.9 copy-start.37
  370.9 5.8 copy-start.31
  370.9 5.8 copy-start.38
  374.5 1.7 copy-start.6
  376.6 13.9 %copy-start.7 = (f32[768,1024]{1,0:T(8,128)S(1)}, f32[768,1024]{1,0:T(8,128)}, u32[]{:S(2)}) copy-start(f32[768,1024]{1,0:T(8,128)} %copy-done.6) | copy-start | bytes 9437188
  376.6 13.9 %copy-start.35 = (f32[4096]{0:T(1024)S(1)}, f32[4096]{0:T(1024)}, u32[]{:S(2)}) copy-start(f32[4096]{0:T(1024)} %param.40) | copy-start | bytes 49156
  418.0 3.1 copy-start.34
  421.2 1.8 copy-start.9
  425.6 51.3 %all-to-all-start.2 = ((bf16[3,256,1024]{1,0,2:T(4,128)(2,1)}), bf16[3,256,1024]{1,0,2:T(4,128)(2,1)S(1)}, u32[]{:S(2)}, u32[]{:S(2)}) async-start(bf16[3,256,1024]{1,0,2:T(4,128)(2,1)} %copy.41), calls=%async_computation.2 | async-start | bytes 4194304 | tf_op jit(solution)/shard_map/all_to_all | solution.py:260
  598.9 5.6 copy-start.8
  598.9 5.6 copy-start.36
  598.9 5.6 copy-start.39
  598.9 143.2 %all-to-all-start.3 = ((bf16[3,1024,3,256]{3,2,0,1:T(4,128)(2,1)}), bf16[3,1024,3,256]{3,2,0,1:T(4,128)(2,1)}, u32[]{:S(2)}, u32[]{:S(2)}) async-start(bf16[3,1024,3,256]{3,2,0,1:T(4,128)(2,1)} %copy.43), calls=%async_computation.3 | async-start | bytes 12582912 | tf_op jit(solution)/shard_map/all_to_all | solution.py:262
  604.4 214.0 %all-reduce.7.cloned.1.call-start = ((), (), s32[]{:S(2)}) async-start(), calls=%async_computation.9 | async-start | bytes 131072 | tf_op jit(solution)/shard_map/psum | solution.py:287
  753.1 9.6 %copy-start.28 = (bf16[4,1024]{1,0:T(4,128)(2,1)S(1)}, bf16[4,1024]{1,0:T(4,128)(2,1)}, u32[]{:S(2)}) copy-start(bf16[4,1024]{1,0:T(4,128)(2,1)} %param.34) | copy-start | bytes 24580
  753.1 11.6 %copy-start.30 = (bf16[4,1024]{1,0:T(4,128)(2,1)S(1)}, bf16[4,1024]{1,0:T(4,128)(2,1)}, u32[]{:S(2)}) copy-start(bf16[4,1024]{1,0:T(4,128)(2,1)} %param.32) | copy-start | bytes 24580
  753.1 13.6 %copy-start.21 = (bf16[768,4]{0,1:T(4,128)(2,1)S(1)}, bf16[768,4]{0,1:T(4,128)(2,1)}, u32[]{:S(2)}) copy-start(bf16[768,4]{0,1:T(4,128)(2,1)} %copy-done.20) | copy-start | bytes 18436
  762.7 6.4 copy-start.19
  762.7 8.7 copy-start.5
  762.7 9.6 %copy-start.25 = (bf16[1024,4]{0,1:T(4,128)(2,1)S(1)}, bf16[1024,4]{0,1:T(4,128)(2,1)}, u32[]{:S(2)}) copy-start(bf16[1024,4]{0,1:T(4,128)(2,1)} %param.31) | copy-start | bytes 24580
  775.5 8.8 copy-start.3
  775.5 8.8 copy-start.10
  775.5 8.8 copy-start.15
  775.5 8.8 copy-start.17
  775.5 8.8 copy-start.23
  787.2 88.9 %all-reduce.5.cloned.1.call-start = ((), (), s32[]{:S(2)}) async-start(), calls=%async_computation.8 | async-start | bytes 131072 | tf_op jit(solution)/shard_map/psum | solution.py:288
Sparse Core Ops, SparseCore 0:
  9.9 48.0 all-gather.4
  59.9 27.8 all-gather.6
  89.7 54.3 all-gather.8
  145.9 54.3 all-gather.10
  787.3 31.0 all-reduce.6
  821.9 54.1 all-reduce.4
